TPU v7x, 32 devices: a whole 2x2x4 slice. The times are simulated.
32 devices in a mesh: seq: 4 (over z), head: 4 (over y, x), rep: 2 (over core).
Axes of the slice: x: 2, y: 2, z: 4, core: 2. Of those that a mesh axis runs over, the one named last changes fastest.
Arguments:
- moe_in: bfloat16 [1024, 2048], P(('rep', 'seq'), 'head'), parts along dimension 0, may hold values from -6 to 6
- grad_out: bfloat16 [1024, 2048], P(('rep', 'seq'), 'head'), parts along dimension 0, may hold values from -6 to 6
- routes: int32 [1024, 8], P(('rep', 'seq')), parts along dimension 0, may hold values from 0 to 63, all different within a row; in each aligned block of 128 rows (0 to 127, 128 to 255, ...) at most 18 rows name the same one
- route_weight: bfloat16 [1024, 8], P(('rep', 'seq')), parts along dimension 0, may hold values from 0.049804688 to 0.5
- w_gate: bfloat16 [64, 2048, 512], P('seq', None, 'head'), may hold values from -0.125 to 0.125
- w_up: bfloat16 [64, 2048, 512], P('seq', None, 'head'), may hold values from -0.125 to 0.125
- w_down: bfloat16 [64, 512, 2048], P('seq', 'head'), may hold values from -0.25 to 0.25
- queries: bfloat16 [1024, 2048], P(('rep', 'seq'), 'head'), parts along dimension 0, may hold values from -8 to 8
- key_value: bfloat16 [1024, 4, 128], P(('rep', 'seq'), 'head'), parts along dimension 0, may hold values from -8 to 8
Outputs:
- d_moe_in: bfloat16 [1024, 2048], P(('rep', 'seq'), 'head'), parts along dimension 0
- d_route_weight: bfloat16 [1024, 8], P(('rep', 'seq')), parts along dimension 0
- grad_gate: bfloat16 [128, 2048, 512], P(('rep', 'seq'), None, 'head'), parts along dimension 0
- grad_up: bfloat16 [128, 2048, 512], P(('rep', 'seq'), None, 'head'), parts along dimension 0
- grad_down: bfloat16 [128, 512, 2048], P(('rep', 'seq'), 'head'), parts along dimension 0
- d_queries: bfloat16 [1024, 2048], P(('rep', 'seq'), 'head'), parts along dimension 0
- d_key_value: bfloat16 [1024, 4, 128], P(('rep', 'seq'), 'head'), parts along dimension 0
There are 2 independent parts, one for each index of `rep`. A program takes and returns all parts, laid end to end along the dimension named above; an argument that names none is the same for every part. Nothing has to cross between parts.
Inputs may be any that keep to these rules, and one draw needn't show every extreme that they name: `routes`: each row names 8 different experts. In each aligned block of 128 rows (the tokens of one sequence shard) no expert is named by more than 18 rows, and in every draw some block has an expert named by exactly 18 rows.
All inputs are finite; a program needn't handle non-finite values.
Results may differ from a plain program's by a relative error of at most 0.03.
Values may be sent and summed in bfloat16 or wider, within the bound.
A program may use at most 128 MiB of HBM per device.

v0:
```python
import jax
import jax.numpy as jnp
from jax import lax
from jax.sharding import PartitionSpec as P

EXPERTS = 64
WIN = 512
CAP = 18


def shifted(block, axis, distance):
    devices = range(lax.axis_size(axis))
    route = [(i - distance, i) for i in devices if i - distance in devices]
    return lax.ppermute(block, axis, route)


def slot_tables(routes, route_weight):
    token_rows, top_count = routes.shape
    flat_expert = routes.reshape(token_rows * top_count)
    expert_ids = jnp.arange(EXPERTS, dtype=jnp.int32)
    one_hot = (flat_expert[:, None] == expert_ids[None, :]).astype(jnp.int32)
    earlier = jnp.cumsum(one_hot, axis=0) - one_hot
    slot_rank = jnp.sum(earlier * one_hot, axis=1)
    target = flat_expert * CAP + slot_rank
    slot_cells = jnp.arange(EXPERTS * CAP, dtype=jnp.int32)
    chosen = (target[None, :] == slot_cells[:, None]).astype(jnp.float32)
    by_token = jnp.sum(chosen.reshape(EXPERTS * CAP, token_rows, top_count), axis=2).astype(
        jnp.bfloat16
    )
    slot_weight = jnp.dot(
        chosen,
        route_weight.reshape(token_rows * top_count).astype(jnp.float32),
        precision=lax.Precision.HIGHEST,
    )
    return (chosen, by_token, slot_weight.astype(jnp.bfloat16).reshape(EXPERTS, CAP))


def place_rows(by_token, source):
    placed = jnp.dot(by_token, source, preferred_element_type=jnp.float32)
    return placed.astype(jnp.bfloat16).reshape(EXPERTS, CAP, source.shape[1])


def fetch_window(own_rows, reach):
    earlier_shards = [shifted(own_rows, "seq", offset) for offset in range(reach, 0, -1)]
    window = jnp.concatenate(earlier_shards + [own_rows], axis=0)
    return window


def return_window(d_window, reach, shard):
    summed = d_window[reach * shard :]
    for offset in range(1, reach + 1):
        begin = (reach - offset) * shard
        summed = summed + shifted(
            d_window[begin : begin + shard].astype(jnp.bfloat16), "seq", -offset
        ).astype(jnp.float32)
    return summed


def shards(moe_in, grad_out, routes, route_weight, w_gate, w_up, w_down, queries, key_value):
    tokens = moe_in.shape[0]
    seq_count = lax.axis_size("seq")
    local_experts = w_gate.shape[0]
    chosen, by_token, slot_weight = slot_tables(routes, route_weight)
    part_in, part_grad, got_weight = (
        lax.all_to_all(
            place_rows(by_token, moe_in), "seq", split_axis=0, concat_axis=0, tiled=True
        ),
        lax.all_to_all(
            place_rows(by_token, grad_out), "seq", split_axis=0, concat_axis=0, tiled=True
        ),
        lax.all_to_all(slot_weight, "seq", split_axis=0, concat_axis=0, tiled=True),
    )
    got_in, got_grad = (
        lax.all_gather(part_in, "head", axis=2, tiled=True),
        lax.all_gather(part_grad, "head", axis=2, tiled=True),
    )
    width = got_in.shape[2]
    rows_in = got_in.reshape(seq_count, local_experts, CAP, width)
    rows_grad = got_grad.reshape(seq_count, local_experts, CAP, width)
    scale_w = got_weight.reshape(seq_count, local_experts, CAP).astype(jnp.float32)[..., None]
    gate_pre = jnp.einsum("secd,edf->secf", rows_in, w_gate, preferred_element_type=jnp.float32)
    up_pre = jnp.einsum("secd,edf->secf", rows_in, w_up, preferred_element_type=jnp.float32)
    back_proj = jnp.einsum("secd,efd->secf", rows_grad, w_down, preferred_element_type=jnp.float32)
    sigmoid_gate = jax.nn.sigmoid(gate_pre)
    silu_gate = gate_pre * sigmoid_gate
    active = silu_gate * up_pre
    route_part = jnp.sum(active * back_proj, axis=3)
    d_active = scale_w * back_proj
    d_gate = (d_active * up_pre * sigmoid_gate * (1.0 + gate_pre * (1.0 - sigmoid_gate))).astype(
        jnp.bfloat16
    )
    d_up = (d_active * silu_gate).astype(jnp.bfloat16)
    weighted = (scale_w * active).astype(jnp.bfloat16)
    rows_back = jnp.einsum("secf,edf->secd", d_gate, w_gate, preferred_element_type=jnp.float32)
    rows_back = rows_back + jnp.einsum(
        "secf,edf->secd", d_up, w_up, preferred_element_type=jnp.float32
    )
    rows_quarter = lax.psum_scatter(
        rows_back.reshape(seq_count * local_experts, CAP, width).astype(jnp.bfloat16),
        "head",
        scatter_dimension=2,
        tiled=True,
    )
    route_sum = lax.psum(route_part, "head").astype(jnp.bfloat16)
    grad_gate = jnp.einsum(
        "secd,secf->edf", rows_in, d_gate, preferred_element_type=jnp.float32
    ).astype(jnp.bfloat16)
    grad_up = jnp.einsum(
        "secd,secf->edf", rows_in, d_up, preferred_element_type=jnp.float32
    ).astype(jnp.bfloat16)
    grad_down = jnp.einsum(
        "secf,secd->efd", weighted, rows_grad, preferred_element_type=jnp.float32
    ).astype(jnp.bfloat16)
    back_rows, back_weight = (
        lax.all_to_all(rows_quarter, "seq", split_axis=0, concat_axis=0, tiled=True),
        lax.all_to_all(
            route_sum.reshape(seq_count * local_experts, CAP),
            "seq",
            split_axis=0,
            concat_axis=0,
            tiled=True,
        ),
    )
    quarter = back_rows.shape[2]
    d_moe_in = jnp.einsum(
        "st,sd->td",
        by_token,
        back_rows.reshape(EXPERTS * CAP, quarter),
        preferred_element_type=jnp.float32,
    ).astype(jnp.bfloat16)
    d_route = jnp.dot(
        back_weight.reshape(EXPERTS * CAP).astype(jnp.float32),
        chosen,
        precision=lax.Precision.HIGHEST,
    )
    d_route_weight = d_route.astype(jnp.bfloat16).reshape(routes.shape)
    head_dim = key_value.shape[2] // 2
    per_group = queries.shape[1] // head_dim
    reach = WIN // tokens
    scale = head_dim ** (-0.5)
    d_hidden = (grad_out.astype(jnp.float32) + d_moe_in.astype(jnp.float32)).astype(jnp.bfloat16)
    query_rows = queries.reshape(tokens * per_group, head_dim)
    grad_rows = d_hidden.reshape(tokens * per_group, head_dim)
    own_rows = key_value.reshape(tokens, 2 * head_dim)
    window = fetch_window(own_rows, reach)
    key_rows = window[:, :head_dim]
    value_rows = window[:, head_dim:]
    contract_last = (((1,), (1,)), ((), ()))
    contract_first = (((0,), (0,)), ((), ()))
    seq_index = lax.axis_index("seq")
    key_pos = (seq_index - reach) * tokens + jnp.arange((reach + 1) * tokens, dtype=jnp.int32)
    row_total = tokens * per_group
    block_rows = min(512, row_total)
    block_count = row_total // block_rows

    def attend_block(index, carry):
        d_window, d_query_all = carry
        begin = (index * block_rows).astype(jnp.int32)
        query_blk = lax.dynamic_slice_in_dim(query_rows, begin, block_rows, 0)
        grad_blk = lax.dynamic_slice_in_dim(grad_rows, begin, block_rows, 0)
        scores = (
            lax.dot_general(query_blk, key_rows, contract_last, preferred_element_type=jnp.float32)
            * scale
        )
        position = (
            seq_index * tokens + (begin + jnp.arange(block_rows, dtype=jnp.int32)) // per_group
        )
        visible = (
            (key_pos[None, :] >= 0)
            & (key_pos[None, :] <= position[:, None])
            & (key_pos[None, :] > position[:, None] - WIN)
        )
        scores = jnp.where(visible, scores, -1e30)
        row_max = jnp.max(scores, axis=1, keepdims=True)
        raised = jnp.exp(scores - row_max)
        probs = raised / jnp.sum(raised, axis=1, keepdims=True)
        d_probs = lax.dot_general(
            grad_blk, value_rows, contract_last, preferred_element_type=jnp.float32
        )
        row_dot = jnp.sum(probs * d_probs, axis=1, keepdims=True)
        d_scores = (probs * (d_probs - row_dot) * scale).astype(jnp.bfloat16)
        probs_low = probs.astype(jnp.bfloat16)
        d_query_blk = jnp.dot(d_scores, key_rows, preferred_element_type=jnp.float32).astype(
            jnp.bfloat16
        )
        d_keys = lax.dot_general(
            d_scores, query_blk, contract_first, preferred_element_type=jnp.float32
        )
        d_values = lax.dot_general(
            probs_low, grad_blk, contract_first, preferred_element_type=jnp.float32
        )
        d_window = d_window + jnp.concatenate([d_keys, d_values], axis=1)
        d_query_all = lax.dynamic_update_slice_in_dim(d_query_all, d_query_blk, begin, 0)
        return (d_window, d_query_all)

    window_start = jnp.zeros(((reach + 1) * tokens, 2 * head_dim), jnp.float32)
    query_start = jnp.zeros((row_total, head_dim), jnp.bfloat16)
    d_window, d_query_all = lax.fori_loop(0, block_count, attend_block, (window_start, query_start))
    d_queries = d_query_all.reshape(tokens, per_group * head_dim)
    d_own = return_window(d_window, reach, tokens)
    d_key_value = d_own.astype(jnp.bfloat16).reshape(tokens, 1, 2 * head_dim)
    return (d_moe_in, d_route_weight, grad_gate, grad_up, grad_down, d_queries, d_key_value)


def solution(mesh):
    in_specs = (
        P(("rep", "seq"), "head"),
        P(("rep", "seq"), "head"),
        P(("rep", "seq"), None),
        P(("rep", "seq"), None),
        P("seq", None, "head"),
        P("seq", None, "head"),
        P("seq", "head", None),
        P(("rep", "seq"), "head"),
        P(("rep", "seq"), "head", None),
    )
    out_specs = (
        P(("rep", "seq"), "head"),
        P(("rep", "seq"), None),
        P(("rep", "seq"), None, "head"),
        P(("rep", "seq"), None, "head"),
        P(("rep", "seq"), "head", None),
        P(("rep", "seq"), "head"),
        P(("rep", "seq"), "head", None),
    )
    return jax.shard_map(shards, mesh=mesh, in_specs=in_specs, out_specs=out_specs, check_vma=False)
```

profile of v0, /device:TPU:0, one launch (start us, length us, event | category | flops | bytes accessed | tf_op | source)
XLA Modules:
  0.0 397.5 jit_solution(16628061853176593459)
XLA Ops:
  7.2 0.8 copy.134
  8.3 18.0 %reduce-window.6 = s32[64,8,128]{2,1,0:T(8,128)S(1)} reduce-window(s32[64,8,128]{2,1,0:T(8,128)S(1)} %fusion.68, s32[]{:T(128)} %constant.146.clone.1), window={size=1x1x128 pad=0_0x0_0x127_0}, to_apply=%region_0.0 | reduce-window | flops 8323072 | bytes 524292 | tf_op jit(solution)/shard_map/reduce-window
  27.0 0.7 multiply_add_fusion.1
  27.8 6.0 %convert_reduce_fusion = bf16[1152,128]{1,0:T(8,128)(2,1)S(1)} fusion(s32[128,8]{0,1:T(8,128)S(1)} %multiply_add_fusion.1), kind=kLoop, calls=%fused_computation.56 | loop fusion | flops 3391488 | bytes 299008 | tf_op jit(solution)/shard_map/reduce_sum | solution.py:27
  33.8 0.4 convolution_convert_fusion.1
  34.2 0.4 reshape.144
  34.6 43.2 %all_to_all.30 = bf16[64,18,512]{2,1,0:T(8,128)(2,1)} all-to-all(bf16[64,18,512]{2,1,0:T(8,128)(2,1)S(1)} %reshape.144), channel_id=1, replica_groups=mesh['seq'=4,'head'=4,'rep'=2] {'seq'}, dimensions={0} | all-to-all | bytes 2359296 | tf_op jit(solution)/shard_map/all_to_all | solution.py:65
  78.0 0.4 convolution_convert_fusion.2
  78.4 0.4 reshape.142
  78.8 39.4 %all_to_all.31 = bf16[64,18,512]{2,1,0:T(8,128)(2,1)} all-to-all(bf16[64,18,512]{2,1,0:T(8,128)(2,1)S(1)} %reshape.142), channel_id=1, replica_groups=mesh['seq'=4,'head'=4,'rep'=2] {'seq'}, dimensions={0} | all-to-all | bytes 2359296 | tf_op jit(solution)/shard_map/all_to_all | solution.py:68
  118.5 0.9 fusion.61
  119.6 8.1 %all_to_all.32 = bf16[4,2,144]{2,1,0:T(2,128)(2,1)S(1)} all-to-all(bf16[4,2,144]{2,1,0:T(2,128)(2,1)S(1)} %reshape.167), channel_id=1, replica_groups=mesh['seq'=4,'head'=4,'rep'=2] {'seq'}, dimensions={0} | all-to-all | bytes 4608 | tf_op jit(solution)/shard_map/all_to_all | solution.py:71
  127.9 19.2 %all-gather.5.cloned.1.call-done = bf16[64,18,2048]{2,1,0:T(8,128)(2,1)} async-done(((bf16[64,18,512]{2,1,0:T(8,128)(2,1)}), bf16[64,18,2048]{2,1,0:T(8,128)(2,1)}) %all-gather.5.cloned.1.call-update) | async-done | bytes 4718608 | tf_op jit(solution)/shard_map/all_gather | solution.py:74
  147.1 7.7 %fusion.46 = f32[4,16,18,128]{3,2,0,1:T(8,128)S(1)} fusion(bf16[16,2048,128]{2,1,0:T(8,128)(2,1)} %param.16, bf16[4,16,18,2048]{3,2,1,0:T(8,128)(2,1)} %bitcast.115), kind=kOutput, calls=%fused_computation.66 | convolution fusion | flops 603979776 | bytes 13697024 | tf_op jit(solution)/shard_map/secd,edf->secf/dot_general | solution.py:82
  154.8 6.9 %fusion.56 = f32[4,16,18,128]{3,2,0,1:T(8,128)S(1)} fusion(bf16[16,2048,128]{2,1,0:T(8,128)(2,1)} %param.15, bf16[4,16,18,2048]{3,2,1,0:T(8,128)(2,1)S(1)} %bitcast.118), kind=kOutput, calls=%fused_computation.68 | convolution fusion | flops 603979776 | bytes 13697024 | tf_op jit(solution)/shard_map/secd,edf->secf/dot_general | solution.py:81
  161.7 57.2 %all-gather.3.cloned.1.call-done = bf16[64,18,2048]{2,1,0:T(8,128)(2,1)} async-done(((bf16[64,18,512]{2,1,0:T(8,128)(2,1)}), bf16[64,18,2048]{2,1,0:T(8,128)(2,1)}) %all-gather.3.cloned.1.call-update) | async-done | bytes 4718608 | tf_op jit(solution)/shard_map/all_gather | solution.py:75
  218.8 8.3 %multiply_reduce_fusion.1 = (f32[4,16,18]{2,0,1:T(4,128)S(1)}, bf16[4,16,18,128]{3,2,0,1:T(8,128)(2,1)S(1)}, bf16[4,16,18,128]{3,2,0,1:T(8,128)(2,1)S(1)}) fusion(f32[4,16,18,128]{3,2,0,1:T(8,128)S(1)} %fusion.46, f32[4,16,18,128]{3,2,0,1:T(8,128)S(1)} %fusion.56, f32[4,16,18]{2,0,1:T(4,128)S(1)} %copy.140, bf16[16,128,2048]{2,1,0:T(8,128)(2,1)} %param.17, ...), kind=kOutput, calls=%fused_computation.72 | convolution fusion | flops 606485376 | bytes 14885888 | tf_op jit(solution)/shard_map/secd,efd->secf/dot_general | solution.py:83
  227.2 13.3 %fusion.23 = f32[16,4,18,2048]{3,2,1,0:T(8,128)} fusion(bf16[4,16,18,128]{3,2,0,1:T(8,128)(2,1)S(1)} %get-tuple-element.334, bf16[16,2048,128]{2,1,0:T(8,128)(2,1)} %param.15), kind=kOutput, calls=%fused_computation.40 | convolution fusion | flops 603979776 | bytes 18120704 | tf_op jit(solution)/shard_map/secf,edf->secd/dot_general | solution.py:94
  240.5 15.1 %fusion.33 = bf16[4,16,18,2048]{3,2,0,1:T(8,128)(2,1)} fusion(f32[16,4,18,2048]{3,2,1,0:T(8,128)} %fusion.23, bf16[4,16,18,128]{3,2,0,1:T(8,128)(2,1)S(1)} %get-tuple-element.335, bf16[16,2048,128]{2,1,0:T(8,128)(2,1)} %param.16), kind=kOutput, calls=%fused_computation.50 | convolution fusion | flops 608698368 | bytes 22839296 | tf_op jit(solution)/shard_map/secf,edf->secd/dot_general | solution.py:95
  255.6 7.6 %copy.146 = bf16[4,16,18,2048]{3,1,0,2:T(8,128)(2,1)} copy(bf16[4,16,18,2048]{3,2,0,1:T(8,128)(2,1)} %fusion.33) | data formatting | bytes 9437184 | tf_op jit(solution)/shard_map/convert_element_type | solution.py:99
  263.1 0.7 copy-done.8
  263.9 0.6 collective-permute-start
  264.5 5.2 %collective-permute-start.1 = (bf16[128,128]{1,0:T(8,128)(2,1)S(1)}, bf16[128,128]{1,0:T(8,128)(2,1)S(1)}, u32[]{:S(2)}, u32[]{:S(2)}) collective-permute-start(bf16[128,128]{1,0:T(8,128)(2,1)S(1)} %bitcast.110), channel_id=1, source_target_pairs={{0,24},{1,25},{2,26},{3,27},{4,28},{5,29},{6,30},{7,31}} | collective-permute-start | bytes 98312 | tf_op jit(solution)/shard_map/ppermute | solution.py:14
  269.8 1.3 collective-permute-start.2
  271.1 2.5 collective-permute-start.3
  273.6 0.9 reshape.149
  274.5 0.6 collective-permute-done.3
  275.1 0.8 fusion.80
  275.9 17.0 %psum.7 = bf16[4,16,18]{2,0,1:T(4,128)(2,1)S(1)} all-reduce(f32[4,16,18]{2,0,1:T(4,128)S(1)} %get-tuple-element.333), channel_id=1, replica_groups=mesh['seq'=4,'head'=4,'rep'=2] {'head'}, use_global_device_ids=true, to_apply=%region_6.7 | all-reduce | flops 1152 | bytes 6912 | tf_op jit(solution)/shard_map/psum | solution.py:104
  292.9 0.7 reshape.169
  293.6 3.6 all-to-all-start.4
  297.2 8.9 %bitcast_convert_fusion = bf16[16,128,2048]{2,1,0:T(8,128)(2,1)} fusion(bf16[4,16,18,2048]{3,2,1,0:T(8,128)(2,1)} %bitcast.107, f32[4,16,18]{2,0,1:T(4,128)S(1)} %copy.140, f32[4,16,18,128]{3,2,0,1:T(8,128)S(1)} %fusion.46, f32[4,16,18,128]{3,2,0,1:T(8,128)S(1)} %fusion.56), kind=kOutput, calls=%fused_computation.36 | convolution fusion | flops 609206272 | bytes 14291456 | tf_op jit(solution)/shard_map/secf,secd->efd/dot_general | solution.py:111
  306.1 15.2 %reduce-scatter.2.cloned.1.call-done = bf16[64,18,512]{2,0,1:T(8,128)(2,1)} async-done(((bf16[64,18,2048]{2,0,1:T(8,128)(2,1)}), bf16[64,18,512]{2,0,1:T(8,128)(2,1)}) %reduce-scatter.2.cloned.1.call-update) | async-done | bytes 1179664 | tf_op jit(solution)/shard_map/reduce_scatter | solution.py:98
  321.3 3.1 copy.147
  324.4 4.6 %all-to-all-start.3 = ((bf16[64,18,512]{2,1,0:T(8,128)(2,1)}), bf16[64,18,512]{2,1,0:T(8,128)(2,1)S(1)}, u32[]{:S(2)}, u32[]{:S(2)}) async-start(bf16[64,18,512]{2,1,0:T(8,128)(2,1)} %copy.147), calls=%async_computation.4 | async-start | bytes 3145728 | tf_op jit(solution)/shard_map/all_to_all | solution.py:115
  329.0 8.8 %bitcast_convert_fusion.1 = bf16[16,2048,128]{2,1,0:T(8,128)(2,1)} fusion(bf16[4,16,18,128]{3,2,0,1:T(8,128)(2,1)S(1)} %get-tuple-element.335, bf16[4,16,18,2048]{3,2,1,0:T(8,128)(2,1)} %bitcast.116), kind=kOutput, calls=%fused_computation.37 | convolution fusion | flops 608174080 | bytes 13402112 | tf_op jit(solution)/shard_map/secd,secf->edf/dot_general | solution.py:108
  337.8 8.8 %bitcast_convert_fusion.2 = bf16[16,2048,128]{2,1,0:T(8,128)(2,1)} fusion(bf16[4,16,18,128]{3,2,0,1:T(8,128)(2,1)S(1)} %copy-done.6, bf16[4,16,18,2048]{3,2,1,0:T(8,128)(2,1)} %bitcast.117), kind=kOutput, calls=%fused_computation.38 | convolution fusion | flops 608174080 | bytes 13402112 | tf_op jit(solution)/shard_map/secd,secf->edf/dot_general | solution.py:105
  346.8 19.0 %all-to-all-done.3 = bf16[64,18,512]{2,1,0:T(8,128)(2,1)S(1)} async-done(((bf16[64,18,512]{2,1,0:T(8,128)(2,1)}), bf16[64,18,512]{2,1,0:T(8,128)(2,1)S(1)}, u32[]{:S(2)}, u32[]{:S(2)}) %all-to-all-start.3) | async-done | bytes 1179680 | tf_op jit(solution)/shard_map/all_to_all | solution.py:115
  365.8 0.4 reshape.146
  366.2 2.0 add_convert_fusion.1
  368.4 10.3 %while.18 = (s32[]{:T(128)}, f32[640,128]{0,1:T(8,128)S(1)}, bf16[1024,64]{0,1:T(8,128)(2,1)S(1)}, s32[]{:T(128)}, bf16[1024,64]{1,0:T(8,128)(2,1)}, /*index=5*/...) while((s32[]{:T(128)}, f32[640,128]{0,1:T(8,128)S(1)}, ...), condition=%wide.region_11.12_spmd.clone, body=%wide.region_7.11_spmd.clone.sunk | while | flops 217212288 | bytes 13930997 | solution.py:198
  368.4 1.6 fusion.121
  370.0 0.4 fusion.122
  370.4 1.5 multiply_reduce_fusion.3
  371.9 0.4 multiply_convert_fusion.6
  372.6 0.5 fusion.123
  373.2 0.3 fusion.125
  373.6 1.6 fusion.121
  375.2 0.4 fusion.122
  375.5 1.5 multiply_reduce_fusion.3
  377.0 0.4 multiply_convert_fusion.6
  377.5 0.3 fusion.124
  377.8 0.5 fusion.123
  378.4 0.3 fusion.125
  378.9 1.3 collective-permute-start.4
  380.2 1.3 collective-permute-start.5
  381.5 1.3 collective-permute-start.6
  382.8 0.7 collective-permute-start.7
  383.5 0.9 fusion.36
  384.5 0.7 copy.155
  385.3 0.9 reshape.152
  386.2 1.0 collective-permute-done.5
  387.2 3.1 collective-permute-done.6
  390.3 0.6 fusion.73
  (80 shorter events, 3.2 us)
Async XLA Ops:
  7.2 26.6 %copy-start = (bf16[128,512]{1,0:T(8,128)(2,1)S(1)}, bf16[128,512]{1,0:T(8,128)(2,1)}, u32[]{:S(2)}) copy-start(bf16[128,512]{1,0:T(8,128)(2,1)} %param.11) | copy-start | bytes 393220
  7.2 139.9 %all-gather.5.cloned.1.call-start = ((), (), s32[]{:S(2)}) async-start(), calls=%async_computation.7 | async-start | bytes 7864320 | tf_op jit(solution)/shard_map/all_gather | solution.py:74
  27.0 51.0 %copy-start.4 = (bf16[128,512]{1,0:T(8,128)(2,1)S(1)}, bf16[128,512]{1,0:T(8,128)(2,1)}, u32[]{:S(2)}) copy-start(bf16[128,512]{1,0:T(8,128)(2,1)} %param.12) | copy-start | bytes 393220
  33.8 44.6 %copy-start.2 = (bf16[1152,128]{1,0:T(8,128)(2,1)}, bf16[1152,128]{1,0:T(8,128)(2,1)S(1)}, u32[]{:S(2)}) copy-start(bf16[1152,128]{1,0:T(8,128)(2,1)S(1)} %convert_reduce_fusion) | copy-start | bytes 884740
  77.9 40.4 %copy-start.9 = (bf16[128,8]{0,1:T(8,128)(2,1)S(1)}, bf16[128,8]{0,1:T(8,128)(2,1)}, u32[]{:S(2)}) copy-start(bf16[128,8]{0,1:T(8,128)(2,1)} %param.14) | copy-start | bytes 6148
  77.9 140.9 %all-gather.3.cloned.1.call-start = ((), (), s32[]{:S(2)}) async-start(), calls=%async_computation.6 | async-start | bytes 7864320 | tf_op jit(solution)/shard_map/all_gather | solution.py:75
  118.2 203.1 %reduce-scatter.2.cloned.1.call-start = ((), (), s32[]{:S(2)}) async-start(), calls=%async_computation.8 | async-start | bytes 5898240 | tf_op jit(solution)/shard_map/reduce_scatter | solution.py:98
  147.1 7.7 %copy-start.10 = (bf16[64,18,2048]{2,1,0:T(8,128)(2,1)S(1)}, bf16[64,18,2048]{2,1,0:T(8,128)(2,1)}, u32[]{:S(2)}) copy-start(bf16[64,18,2048]{2,1,0:T(8,128)(2,1)} %all-gather.5.cloned.1.call-done) | copy-start | bytes 14155780
  227.2 13.3 %copy-start.5 = (bf16[4,16,18,128]{3,2,0,1:T(8,128)(2,1)}, bf16[4,16,18,128]{3,2,0,1:T(8,128)(2,1)S(1)}, u32[]{:S(2)}) copy-start(bf16[4,16,18,128]{3,2,0,1:T(8,128)(2,1)S(1)} %get-tuple-element.334) | copy-start | bytes 884740
  263.1 0.8 copy-start.8
  263.1 10.4 %copy-start.7 = (bf16[128,512]{1,0:T(8,128)(2,1)S(1)}, bf16[128,512]{1,0:T(8,128)(2,1)}, u32[]{:S(2)}) copy-start(bf16[128,512]{1,0:T(8,128)(2,1)} %param.18) | copy-start | bytes 393220
  263.9 10.6 %collective-permute-start = (bf16[128,128]{1,0:T(8,128)(2,1)S(1)}, bf16[128,128]{1,0:T(8,128)(2,1)S(1)}, u32[]{:S(2)}, u32[]{:S(2)}) collective-permute-start(bf16[128,128]{1,0:T(8,128)(2,1)S(1)} %bitcast.109), channel_id=1, source_target_pairs={} | collective-permute-start | bytes 98312 | tf_op jit(solution)/shard_map/ppermute | solution.py:14
  264.5 10.0 %collective-permute-start.1 = (bf16[128,128]{1,0:T(8,128)(2,1)S(1)}, bf16[128,128]{1,0:T(8,128)(2,1)S(1)}, u32[]{:S(2)}, u32[]{:S(2)}) collective-permute-start(bf16[128,128]{1,0:T(8,128)(2,1)S(1)} %bitcast.110), channel_id=1, source_target_pairs={{0,24},{1,25},{2,26},{3,27},{4,28},{5,29},{6,30},{7,31}} | collective-permute-start | bytes 98312 | tf_op jit(solution)/shard_map/ppermute | solution.py:14
  269.8 4.7 %collective-permute-start.2 = (bf16[128,128]{1,0:T(8,128)(2,1)S(1)}, bf16[128,128]{1,0:T(8,128)(2,1)S(1)}, u32[]{:S(2)}, u32[]{:S(2)}) collective-permute-start(bf16[128,128]{1,0:T(8,128)(2,1)S(1)} %bitcast.111), channel_id=1, source_target_pairs={{0,16},{8,24},{1,17},{9,25},{2,18},{10,26},{3,19},{11,27},{4,20},{... | collective-permute-start | bytes 98312 | tf_op jit(solution)/shard_map/ppermute | solution.py:14
  271.1 4.1 %collective-permute-start.3 = (bf16[128,128]{1,0:T(8,128)(2,1)S(1)}, bf16[128,128]{1,0:T(8,128)(2,1)S(1)}, u32[]{:S(2)}, u32[]{:S(2)}) collective-permute-start(bf16[128,128]{1,0:T(8,128)(2,1)S(1)} %bitcast.112), channel_id=1, source_target_pairs={{0,8},{8,16},{16,24},{1,9},{9,17},{17,25},{2,10},{10,18},{18,26},{... | collective-permute-start | bytes 98312 | tf_op jit(solution)/shard_map/ppermute | solution.py:14
  293.6 30.8 %all-to-all-start.4 = ((bf16[4,2,144]{2,1,0:T(2,128)(2,1)}), bf16[4,2,144]{2,1,0:T(2,128)(2,1)S(1)}, u32[]{:S(2)}, u32[]{:S(2)}) async-start(bf16[4,2,144]{2,1,0:T(2,128)(2,1)} %reshape.169), calls=%async_computation.5 | async-start | bytes 8192 | tf_op jit(solution)/shard_map/all_to_all | solution.py:116
  324.4 41.4 %all-to-all-start.3 = ((bf16[64,18,512]{2,1,0:T(8,128)(2,1)}), bf16[64,18,512]{2,1,0:T(8,128)(2,1)S(1)}, u32[]{:S(2)}, u32[]{:S(2)}) async-start(bf16[64,18,512]{2,1,0:T(8,128)(2,1)} %copy.147), calls=%async_computation.4 | async-start | bytes 3145728 | tf_op jit(solution)/shard_map/all_to_all | solution.py:115
  329.0 8.8 %copy-start.6 = (bf16[4,16,18,128]{3,2,0,1:T(8,128)(2,1)S(1)}, bf16[4,16,18,128]{3,2,0,1:T(8,128)(2,1)}, u32[]{:S(2)}) copy-start(bf16[4,16,18,128]{3,2,0,1:T(8,128)(2,1)} %copy-done.5) | copy-start | bytes 884740
  370.4 2.0 copy-start.3
  375.5 2.0 copy-start.3
  378.7 12.3 %copy-start.1 = (bf16[128,512]{1,0:T(8,128)(2,1)S(1)}, bf16[128,512]{1,0:T(8,128)(2,1)}, u32[]{:S(2)}) copy-start(bf16[128,512]{1,0:T(8,128)(2,1)} %param.11) | copy-start | bytes 393220
  378.9 7.3 %collective-permute-start.4 = (bf16[128,128]{1,0:T(8,128)(2,1)S(1)}, bf16[128,128]{1,0:T(8,128)(2,1)S(1)}, u32[]{:S(2)}, u32[]{:S(2)}) collective-permute-start(bf16[128,128]{1,0:T(8,128)(2,1)S(1)} %get-tuple-element.336), channel_id=1, source_target_pairs={{8,0},{16,8},{24,16},{9,1},{17,9},{25,17},{10,2},{18,10},{26,18},{... | collective-permute-start | bytes 98312 | tf_op jit(solution)/shard_map/ppermute | solution.py:14
  380.2 7.0 %collective-permute-start.5 = (bf16[128,128]{1,0:T(8,128)(2,1)S(1)}, bf16[128,128]{1,0:T(8,128)(2,1)S(1)}, u32[]{:S(2)}, u32[]{:S(2)}) collective-permute-start(bf16[128,128]{1,0:T(8,128)(2,1)S(1)} %get-tuple-element.339), channel_id=1, source_target_pairs={{16,0},{24,8},{17,1},{25,9},{18,2},{26,10},{19,3},{27,11},{20,4},{... | collective-permute-start | bytes 98312 | tf_op jit(solution)/shard_map/ppermute | solution.py:14
  381.5 8.8 %collective-permute-start.6 = (bf16[128,128]{1,0:T(8,128)(2,1)S(1)}, bf16[128,128]{1,0:T(8,128)(2,1)S(1)}, u32[]{:S(2)}, u32[]{:S(2)}) collective-permute-start(bf16[128,128]{1,0:T(8,128)(2,1)S(1)} %get-tuple-element.338), channel_id=1, source_target_pairs={{24,0},{25,1},{26,2},{27,3},{28,4},{29,5},{30,6},{31,7}} | collective-permute-start | bytes 98312 | tf_op jit(solution)/shard_map/ppermute | solution.py:14
  382.8 7.5 %collective-permute-start.7 = (bf16[128,128]{1,0:T(8,128)(2,1)S(1)}, bf16[128,128]{1,0:T(8,128)(2,1)S(1)}, u32[]{:S(2)}, u32[]{:S(2)}) collective-permute-start(bf16[128,128]{1,0:T(8,128)(2,1)S(1)} %get-tuple-element.337), channel_id=1, source_target_pairs={} | collective-permute-start | bytes 98312 | tf_op jit(solution)/shard_map/ppermute | solution.py:14
Sparse Core Ops, SparseCore 0:
  78.0 69.0 all-gather.4
  148.9 69.8 all-gather.2
  263.3 58.0 reduce-scatter.1
where the time goes:
time: 398 us; the launch traced here: 397 us
  waiting for transfers between devices  115 us (29%)
  blocking collectives  108 us (27%)
  matrix products  90.7 us (23%)
  other arithmetic  27.5 us (7%)
  starting transfers between devices  22.5 us (6%)
  local copies, waits for them, and re-layouts  19.5 us (5%)
  between operations  14.2 us (4%)
    all_gather x1, waiting for transfers between devices, shards(): lax.all_gather(part_grad, 'head', axis=2, tiled=True)  57.2 us
    all_to_all x1, blocking collectives, shards(): lax.all_to_all(place_rows(by_token, moe_in), 'seq', split_axis=0, concat_...  43.2 us
    all_to_all x1, blocking collectives, shards(): lax.all_to_all(place_rows(by_token, grad_out), 'seq', split_axis=0, conca...  39.4 us
    all_gather x1, waiting for transfers between devices, shards(): lax.all_gather(part_in, 'head', axis=2, tiled=True)  19.2 us
    all_to_all x1, waiting for transfers between devices, shards(): lax.all_to_all(rows_quarter, 'seq', split_axis=0, concat_axis=0, tiled=True)  19 us
    another operation x4, other arithmetic  18.2 us
    psum x1, blocking collectives, shards(): route_sum = lax.psum(route_part, 'head').astype(jnp.bfloat16)  17 us
    reduce_scatter x1, waiting for transfers between devices, shards(): lax.psum_scatter(rows_back.reshape(seq_count * local_experts, CAP, width)...  15.2 us
  transfers between devices with their start and end apart: 13, of which 7 were waited for; matrix products, arithmetic and copies ran while one was open for 13% of the time, Pallas kernels for 0%

commit v1 on v0

--- a/solution.py
+++ b/solution.py
@@ -72,7 +72,7 @@
     )
     got_in, got_grad = (
         lax.all_gather(part_in, "head", axis=2, tiled=True),
-        lax.all_gather(part_grad, "head", axis=2, tiled=True),
+        jnp.concatenate(lax.all_gather(part_grad, "head"), axis=2),
     )
     width = got_in.shape[2]
     rows_in = got_in.reshape(seq_count, local_experts, CAP, width)

time: 398 us -> 414 us (1.040); the launches traced: 397 us -> 408 us
  local copies, waits for them, and re-layouts: 19.5 us -> 39.4 us
  waiting for transfers between devices: 115 us -> 97.7 us
  matrix products: 90.7 us -> 97.6 us
    all_gather x1, waiting for transfers between devices: 57.2 us -> 45 us  [shards(): lax.all_gather(part_grad, 'head')]
    another operation x2 -> x3, local copies, waits for them, and re-layouts: 0.09 us -> 8.98 us  [the longest x1 8.89 us: shards(): rows_grad = got_grad.reshape(seq_count, local_experts, CAP, width)]
    all_gather x0 -> x1, local copies, waits for them, and re-layouts: none -> 8.61 us  [shards(): lax.all_gather(part_grad, 'head')]
  transfers between devices with their start and end apart: 13 -> 13, of which waited for: 7 -> 7; matrix products, arithmetic and copies ran while one was open for 13% -> 14% of each run, Pallas kernels for 0% -> 0%
where the time goes in v1:
time: 414 us; the launch traced here: 408 us
  blocking collectives  108 us (26%)
  waiting for transfers between devices  97.7 us (24%)
  matrix products  97.6 us (24%)
  local copies, waits for them, and re-layouts  39.4 us (10%)
  other arithmetic  27.5 us (7%)
  starting transfers between devices  22.8 us (6%)
  between operations  14.6 us (4%)
    all_gather x1, waiting for transfers between devices, shards(): lax.all_gather(part_grad, 'head')  45 us
    all_to_all x1, blocking collectives, shards(): lax.all_to_all(place_rows(by_token, moe_in), 'seq', split_axis=0, concat_...  43.2 us
    all_to_all x1, blocking collectives, shards(): lax.all_to_all(place_rows(by_token, grad_out), 'seq', split_axis=0, conca...  39.1 us
    all_to_all x1, waiting for transfers between devices, shards(): lax.all_to_all(rows_quarter, 'seq', split_axis=0, concat_axis=0, tiled=True)  18.9 us
    another operation x4, other arithmetic  18.2 us
    all_gather x1, waiting for transfers between devices, shards(): lax.all_gather(part_in, 'head', axis=2, tiled=True)  17.7 us
    psum x1, blocking collectives, shards(): route_sum = lax.psum(route_part, 'head').astype(jnp.bfloat16)  17 us
    dot_general x1, matrix products, shards(): jnp.einsum('secf,edf->secd', d_up, w_up, preferred_element_type=jnp.float32)  14.9 us
  transfers between devices with their start and end apart: 13, of which 7 were waited for; matrix products, arithmetic and copies ran while one was open for 14% of the time, Pallas kernels for 0%

profile of v1, /device:TPU:0, one launch (start us, length us, event | category | flops | bytes accessed | tf_op | source)
XLA Modules:
  0.0 407.5 jit_solution(16230475000738614973)
XLA Ops:
  7.2 0.8 copy.138
  8.3 18.0 %reduce-window.6 = s32[64,8,128]{2,1,0:T(8,128)S(1)} reduce-window(s32[64,8,128]{2,1,0:T(8,128)S(1)} %fusion.68, s32[]{:T(128)} %constant.146.clone.1), window={size=1x1x128 pad=0_0x0_0x127_0}, to_apply=%region_0.0 | reduce-window | flops 8323072 | bytes 524292 | tf_op jit(solution)/shard_map/reduce-window
  27.0 0.7 multiply_add_fusion.1
  27.8 6.0 %convert_reduce_fusion = bf16[1152,128]{1,0:T(8,128)(2,1)S(1)} fusion(s32[128,8]{0,1:T(8,128)S(1)} %multiply_add_fusion.1), kind=kLoop, calls=%fused_computation.57 | loop fusion | flops 3391488 | bytes 299008 | tf_op jit(solution)/shard_map/reduce_sum | solution.py:27
  33.8 0.5 convolution_convert_fusion.1
  34.2 0.4 reshape.144
  34.6 43.2 %all_to_all.30 = bf16[64,18,512]{2,1,0:T(8,128)(2,1)} all-to-all(bf16[64,18,512]{2,1,0:T(8,128)(2,1)S(1)} %reshape.144), channel_id=1, replica_groups=mesh['seq'=4,'head'=4,'rep'=2] {'seq'}, dimensions={0} | all-to-all | bytes 2359296 | tf_op jit(solution)/shard_map/all_to_all | solution.py:65
  77.9 0.4 convolution_convert_fusion.2
  78.4 0.4 reshape.142
  78.8 39.1 %all_to_all.31 = bf16[64,18,512]{2,1,0:T(8,128)(2,1)S(1)} all-to-all(bf16[64,18,512]{2,1,0:T(8,128)(2,1)S(1)} %reshape.142), channel_id=1, replica_groups=mesh['seq'=4,'head'=4,'rep'=2] {'seq'}, dimensions={0} | all-to-all | bytes 2359296 | tf_op jit(solution)/shard_map/all_to_all | solution.py:68
  117.9 1.4 copy.145
  119.6 0.9 fusion.61
  120.7 8.6 %all_to_all.32 = bf16[4,2,144]{2,1,0:T(2,128)(2,1)S(1)} all-to-all(bf16[4,2,144]{2,1,0:T(2,128)(2,1)S(1)} %reshape.168), channel_id=1, replica_groups=mesh['seq'=4,'head'=4,'rep'=2] {'seq'}, dimensions={0} | all-to-all | bytes 4608 | tf_op jit(solution)/shard_map/all_to_all | solution.py:71
  129.4 17.7 %all-gather.4.cloned.1.call-done = bf16[64,18,2048]{2,1,0:T(8,128)(2,1)} async-done(((bf16[64,18,512]{2,1,0:T(8,128)(2,1)}), bf16[64,18,2048]{2,1,0:T(8,128)(2,1)}) %all-gather.4.cloned.1.call-update) | async-done | bytes 4718608 | tf_op jit(solution)/shard_map/all_gather | solution.py:74
  147.1 7.7 %fusion.46 = f32[4,16,18,128]{3,2,0,1:T(8,128)S(1)} fusion(bf16[16,2048,128]{2,1,0:T(8,128)(2,1)} %param.16, bf16[4,16,18,2048]{3,2,1,0:T(8,128)(2,1)} %bitcast.118), kind=kOutput, calls=%fused_computation.67 | convolution fusion | flops 603979776 | bytes 13697024 | tf_op jit(solution)/shard_map/secd,edf->secf/dot_general | solution.py:82
  154.8 6.7 %fusion.56 = f32[4,16,18,128]{3,2,0,1:T(8,128)S(1)} fusion(bf16[16,2048,128]{2,1,0:T(8,128)(2,1)} %param.15, bf16[4,16,18,2048]{3,2,1,0:T(8,128)(2,1)S(1)} %bitcast.121), kind=kOutput, calls=%fused_computation.69 | convolution fusion | flops 603979776 | bytes 13697024 | tf_op jit(solution)/shard_map/secd,edf->secf/dot_general | solution.py:81
  161.5 45.0 %all-gather.6.cloned.1.call-done = bf16[256,18,512]{2,0,1:T(8,128)(2,1)} async-done(((bf16[64,18,512]{2,0,1:T(8,128)(2,1)}), bf16[256,18,512]{2,0,1:T(8,128)(2,1)}) %all-gather.6.cloned.1.call-update) | async-done | bytes 4718608 | tf_op jit(solution)/shard_map/all_gather | solution.py:75
  206.5 8.6 %copy.194 = bf16[4,64,18,512]{3,0,1,2:T(4,128)(2,1)} copy(bf16[4,64,18,512]{3,1,0,2:T(8,128)(2,1)} %bitcast.110) | data formatting | bytes 9437184 | tf_op jit(solution)/shard_map/all_gather | solution.py:75
  215.1 8.9 %reshape_reshape.3 = bf16[4,16,18,2048]{3,1,0,2:T(8,128)(2,1)} reshape(bf16[64,18,4,512]{3,2,0,1:T(4,128)(2,1)} %bitcast.108) | data formatting | bytes 9437184 | tf_op jit(solution)/shard_map/reshape;reshape | solution.py:79
  224.0 9.6 %multiply_reduce_fusion.1 = (f32[4,16,18]{2,0,1:T(4,128)S(1)}, bf16[4,16,18,128]{3,2,0,1:T(8,128)(2,1)S(1)}, bf16[4,16,18,128]{3,2,0,1:T(8,128)(2,1)S(1)}) fusion(f32[4,16,18,128]{3,2,0,1:T(8,128)S(1)} %fusion.46, f32[4,16,18,128]{3,2,0,1:T(8,128)S(1)} %fusion.56, f32[4,16,18]{2,0,1:T(4,128)S(1)} %copy.144, bf16[16,128,2048]{2,1,0:T(8,128)(2,1)} %param.17, ...), kind=kOutput, calls=%fused_computation.73 | convolution fusion | flops 606485376 | bytes 14885888 | tf_op jit(solution)/shard_map/secd,efd->secf/dot_general | solution.py:83
  233.6 13.4 %fusion.23 = f32[16,4,18,2048]{3,2,1,0:T(8,128)} fusion(bf16[4,16,18,128]{3,2,0,1:T(8,128)(2,1)S(1)} %get-tuple-element.334, bf16[16,2048,128]{2,1,0:T(8,128)(2,1)} %param.15), kind=kOutput, calls=%fused_computation.40 | convolution fusion | flops 603979776 | bytes 18120704 | tf_op jit(solution)/shard_map/secf,edf->secd/dot_general | solution.py:94
  247.1 14.9 %fusion.35 = bf16[4,16,18,2048]{3,2,0,1:T(8,128)(2,1)} fusion(f32[16,4,18,2048]{3,2,1,0:T(8,128)} %fusion.23, bf16[4,16,18,128]{3,2,0,1:T(8,128)(2,1)S(1)} %get-tuple-element.335, bf16[16,2048,128]{2,1,0:T(8,128)(2,1)} %param.16), kind=kOutput, calls=%fused_computation.52 | convolution fusion | flops 608698368 | bytes 22839296 | tf_op jit(solution)/shard_map/secf,edf->secd/dot_general | solution.py:95
  261.9 7.8 %copy.151 = bf16[4,16,18,2048]{3,1,0,2:T(8,128)(2,1)} copy(bf16[4,16,18,2048]{3,2,0,1:T(8,128)(2,1)} %fusion.35) | data formatting | bytes 9437184 | tf_op jit(solution)/shard_map/convert_element_type | solution.py:99
  269.7 0.7 copy-done.8
  270.5 0.6 collective-permute-start
  271.1 5.2 %collective-permute-start.1 = (bf16[128,128]{1,0:T(8,128)(2,1)S(1)}, bf16[128,128]{1,0:T(8,128)(2,1)S(1)}, u32[]{:S(2)}, u32[]{:S(2)}) collective-permute-start(bf16[128,128]{1,0:T(8,128)(2,1)S(1)} %bitcast.113), channel_id=1, source_target_pairs={{0,24},{1,25},{2,26},{3,27},{4,28},{5,29},{6,30},{7,31}} | collective-permute-start | bytes 98312 | tf_op jit(solution)/shard_map/ppermute | solution.py:14
  276.4 1.3 collective-permute-start.2
  277.7 2.5 collective-permute-start.3
  280.2 0.9 reshape.149
  281.1 0.6 collective-permute-done.3
  281.7 0.8 fusion.80
  282.5 17.0 %psum.7 = bf16[4,16,18]{2,0,1:T(4,128)(2,1)S(1)} all-reduce(f32[4,16,18]{2,0,1:T(4,128)S(1)} %get-tuple-element.333), channel_id=1, replica_groups=mesh['seq'=4,'head'=4,'rep'=2] {'head'}, use_global_device_ids=true, to_apply=%region_6.7 | all-reduce | flops 1152 | bytes 6912 | tf_op jit(solution)/shard_map/psum | solution.py:104
  299.5 0.7 reshape.170
  300.2 3.6 all-to-all-start.4
  303.8 12.7 %bitcast_convert_fusion = bf16[16,128,2048]{2,1,0:T(8,128)(2,1)} fusion(bf16[4,16,18,2048]{3,1,0,2:T(8,128)(2,1)} %reshape_reshape.3, f32[4,16,18]{2,0,1:T(4,128)S(1)} %copy.144, f32[4,16,18,128]{3,2,0,1:T(8,128)S(1)} %fusion.46, f32[4,16,18,128]{3,2,0,1:T(8,128)S(1)} %fusion.56), kind=kOutput, calls=%fused_computation.36 | convolution fusion | flops 609206272 | bytes 14291456 | tf_op jit(solution)/shard_map/secf,secd->efd/dot_general | solution.py:111
  316.5 11.4 %reduce-scatter.2.cloned.1.call-done = bf16[64,18,512]{2,0,1:T(8,128)(2,1)} async-done(((bf16[64,18,2048]{2,0,1:T(8,128)(2,1)}), bf16[64,18,512]{2,0,1:T(8,128)(2,1)}) %reduce-scatter.2.cloned.1.call-update) | async-done | bytes 1179664 | tf_op jit(solution)/shard_map/reduce_scatter | solution.py:98
  327.9 3.1 copy.152
  331.0 4.9 %all-to-all-start.3 = ((bf16[64,18,512]{2,1,0:T(8,128)(2,1)}), bf16[64,18,512]{2,1,0:T(8,128)(2,1)S(1)}, u32[]{:S(2)}, u32[]{:S(2)}) async-start(bf16[64,18,512]{2,1,0:T(8,128)(2,1)} %copy.152), calls=%async_computation.4 | async-start | bytes 3145728 | tf_op jit(solution)/shard_map/all_to_all | solution.py:115
  335.9 8.8 %bitcast_convert_fusion.1 = bf16[16,2048,128]{2,1,0:T(8,128)(2,1)} fusion(bf16[4,16,18,128]{3,2,0,1:T(8,128)(2,1)S(1)} %copy-done.4, bf16[4,16,18,2048]{3,2,1,0:T(8,128)(2,1)} %bitcast.119), kind=kOutput, calls=%fused_computation.37 | convolution fusion | flops 608174080 | bytes 13402112 | tf_op jit(solution)/shard_map/secd,secf->edf/dot_general | solution.py:108
  344.7 8.8 %bitcast_convert_fusion.2 = bf16[16,2048,128]{2,1,0:T(8,128)(2,1)} fusion(bf16[4,16,18,128]{3,2,0,1:T(8,128)(2,1)S(1)} %copy-done.6, bf16[4,16,18,2048]{3,2,1,0:T(8,128)(2,1)} %bitcast.120), kind=kOutput, calls=%fused_computation.38 | convolution fusion | flops 608174080 | bytes 13402112 | tf_op jit(solution)/shard_map/secd,secf->edf/dot_general | solution.py:105
  353.7 18.9 %all-to-all-done.3 = bf16[64,18,512]{2,1,0:T(8,128)(2,1)S(1)} async-done(((bf16[64,18,512]{2,1,0:T(8,128)(2,1)}), bf16[64,18,512]{2,1,0:T(8,128)(2,1)S(1)}, u32[]{:S(2)}, u32[]{:S(2)}) %all-to-all-start.3) | async-done | bytes 1179680 | tf_op jit(solution)/shard_map/all_to_all | solution.py:115
  372.6 1.2 reshape.146
  373.8 2.3 add_convert_fusion.1
  376.3 12.0 %while.18 = (s32[]{:T(128)}, f32[640,128]{0,1:T(8,128)S(1)}, bf16[1024,64]{0,1:T(8,128)(2,1)S(1)}, s32[]{:T(128)}, bf16[1024,64]{1,0:T(8,128)(2,1)}, /*index=5*/...) while((s32[]{:T(128)}, f32[640,128]{0,1:T(8,128)S(1)}, ...), condition=%wide.region_11.12_spmd.clone, body=%wide.region_7.11_spmd.clone.sunk | while | flops 217212288 | bytes 13406681 | solution.py:198
  376.4 1.6 fusion.121
  378.3 1.5 multiply_reduce_fusion.3
  379.8 0.4 multiply_convert_fusion.6
  380.2 1.2 fusion.124
  381.4 0.5 fusion.123
  382.4 1.6 fusion.121
  384.3 1.5 multiply_reduce_fusion.3
  385.8 0.4 multiply_convert_fusion.6
  386.2 1.2 fusion.124
  387.4 0.5 fusion.123
  388.5 1.3 collective-permute-start.4
  389.8 1.3 collective-permute-start.5
  391.1 1.3 collective-permute-start.6
  392.4 0.7 collective-permute-start.7
  393.1 0.9 fusion.36
  394.1 0.7 copy.160
  394.9 0.9 reshape.152
  395.8 1.0 collective-permute-done.5
  396.9 3.1 collective-permute-done.6
  399.9 0.6 fusion.73
  (81 shorter events, 4.3 us)
Async XLA Ops:
  7.2 26.6 %copy-start = (bf16[128,512]{1,0:T(8,128)(2,1)S(1)}, bf16[128,512]{1,0:T(8,128)(2,1)}, u32[]{:S(2)}) copy-start(bf16[128,512]{1,0:T(8,128)(2,1)} %param.11) | copy-start | bytes 393220
  7.2 139.9 %all-gather.4.cloned.1.call-start = ((), (), s32[]{:S(2)}) async-start(), calls=%async_computation.6 | async-start | bytes 7864320 | tf_op jit(solution)/shard_map/all_gather | solution.py:74
  27.0 50.9 %copy-start.2 = (bf16[128,512]{1,0:T(8,128)(2,1)S(1)}, bf16[128,512]{1,0:T(8,128)(2,1)}, u32[]{:S(2)}) copy-start(bf16[128,512]{1,0:T(8,128)(2,1)} %param.12) | copy-start | bytes 393220
  77.9 128.6 %all-gather.6.cloned.1.call-start = ((), (), s32[]{:S(2)}) async-start(), calls=%async_computation.8 | async-start | bytes 5898240 | tf_op jit(solution)/shard_map/all_gather | solution.py:75
  78.4 41.0 %copy-start.9 = (bf16[128,8]{0,1:T(8,128)(2,1)S(1)}, bf16[128,8]{0,1:T(8,128)(2,1)}, u32[]{:S(2)}) copy-start(bf16[128,8]{0,1:T(8,128)(2,1)} %param.14) | copy-start | bytes 6148
  119.3 208.6 %reduce-scatter.2.cloned.1.call-start = ((), (), s32[]{:S(2)}) async-start(), calls=%async_computation.7 | async-start | bytes 5898240 | tf_op jit(solution)/shard_map/reduce_scatter | solution.py:98
  147.1 7.7 %copy-start.10 = (bf16[64,18,2048]{2,1,0:T(8,128)(2,1)S(1)}, bf16[64,18,2048]{2,1,0:T(8,128)(2,1)}, u32[]{:S(2)}) copy-start(bf16[64,18,2048]{2,1,0:T(8,128)(2,1)} %all-gather.4.cloned.1.call-done) | copy-start | bytes 14155780
  233.6 13.4 %copy-start.5 = (bf16[4,16,18,128]{3,2,0,1:T(8,128)(2,1)}, bf16[4,16,18,128]{3,2,0,1:T(8,128)(2,1)S(1)}, u32[]{:S(2)}) copy-start(bf16[4,16,18,128]{3,2,0,1:T(8,128)(2,1)S(1)} %get-tuple-element.334) | copy-start | bytes 884740
  233.6 13.4 %copy-start.3 = (bf16[4,16,18,128]{3,2,0,1:T(8,128)(2,1)}, bf16[4,16,18,128]{3,2,0,1:T(8,128)(2,1)S(1)}, u32[]{:S(2)}) copy-start(bf16[4,16,18,128]{3,2,0,1:T(8,128)(2,1)S(1)} %get-tuple-element.335) | copy-start | bytes 884740
  269.7 0.8 copy-start.8
  269.7 10.4 %copy-start.7 = (bf16[128,512]{1,0:T(8,128)(2,1)S(1)}, bf16[128,512]{1,0:T(8,128)(2,1)}, u32[]{:S(2)}) copy-start(bf16[128,512]{1,0:T(8,128)(2,1)} %param.18) | copy-start | bytes 393220
  270.5 10.6 %collective-permute-start = (bf16[128,128]{1,0:T(8,128)(2,1)S(1)}, bf16[128,128]{1,0:T(8,128)(2,1)S(1)}, u32[]{:S(2)}, u32[]{:S(2)}) collective-permute-start(bf16[128,128]{1,0:T(8,128)(2,1)S(1)} %bitcast.112), channel_id=1, source_target_pairs={} | collective-permute-start | bytes 98312 | tf_op jit(solution)/shard_map/ppermute | solution.py:14
  271.1 10.0 %collective-permute-start.1 = (bf16[128,128]{1,0:T(8,128)(2,1)S(1)}, bf16[128,128]{1,0:T(8,128)(2,1)S(1)}, u32[]{:S(2)}, u32[]{:S(2)}) collective-permute-start(bf16[128,128]{1,0:T(8,128)(2,1)S(1)} %bitcast.113), channel_id=1, source_target_pairs={{0,24},{1,25},{2,26},{3,27},{4,28},{5,29},{6,30},{7,31}} | collective-permute-start | bytes 98312 | tf_op jit(solution)/shard_map/ppermute | solution.py:14
  276.4 4.7 %collective-permute-start.2 = (bf16[128,128]{1,0:T(8,128)(2,1)S(1)}, bf16[128,128]{1,0:T(8,128)(2,1)S(1)}, u32[]{:S(2)}, u32[]{:S(2)}) collective-permute-start(bf16[128,128]{1,0:T(8,128)(2,1)S(1)} %bitcast.114), channel_id=1, source_target_pairs={{0,16},{8,24},{1,17},{9,25},{2,18},{10,26},{3,19},{11,27},{4,20},{... | collective-permute-start | bytes 98312 | tf_op jit(solution)/shard_map/ppermute | solution.py:14
  277.7 4.1 collective-permute-start.3
  300.2 30.8 %all-to-all-start.4 = ((bf16[4,2,144]{2,1,0:T(2,128)(2,1)}), bf16[4,2,144]{2,1,0:T(2,128)(2,1)S(1)}, u32[]{:S(2)}, u32[]{:S(2)}) async-start(bf16[4,2,144]{2,1,0:T(2,128)(2,1)} %reshape.170), calls=%async_computation.5 | async-start | bytes 8192 | tf_op jit(solution)/shard_map/all_to_all | solution.py:116
  316.5 19.4 %copy-start.4 = (bf16[4,16,18,128]{3,2,0,1:T(8,128)(2,1)S(1)}, bf16[4,16,18,128]{3,2,0,1:T(8,128)(2,1)}, u32[]{:S(2)}) copy-start(bf16[4,16,18,128]{3,2,0,1:T(8,128)(2,1)} %copy-done.3) | copy-start | bytes 884740
  331.0 41.7 %all-to-all-start.3 = ((bf16[64,18,512]{2,1,0:T(8,128)(2,1)}), bf16[64,18,512]{2,1,0:T(8,128)(2,1)S(1)}, u32[]{:S(2)}, u32[]{:S(2)}) async-start(bf16[64,18,512]{2,1,0:T(8,128)(2,1)} %copy.152), calls=%async_computation.4 | async-start | bytes 3145728 | tf_op jit(solution)/shard_map/all_to_all | solution.py:115
  335.9 8.8 %copy-start.6 = (bf16[4,16,18,128]{3,2,0,1:T(8,128)(2,1)S(1)}, bf16[4,16,18,128]{3,2,0,1:T(8,128)(2,1)}, u32[]{:S(2)}) copy-start(bf16[4,16,18,128]{3,2,0,1:T(8,128)(2,1)} %copy-done.5) | copy-start | bytes 884740
  388.3 12.3 %copy-start.1 = (bf16[128,512]{1,0:T(8,128)(2,1)S(1)}, bf16[128,512]{1,0:T(8,128)(2,1)}, u32[]{:S(2)}) copy-start(bf16[128,512]{1,0:T(8,128)(2,1)} %param.11) | copy-start | bytes 393220
  388.5 7.3 %collective-permute-start.4 = (bf16[128,128]{1,0:T(8,128)(2,1)S(1)}, bf16[128,128]{1,0:T(8,128)(2,1)S(1)}, u32[]{:S(2)}, u32[]{:S(2)}) collective-permute-start(bf16[128,128]{1,0:T(8,128)(2,1)S(1)} %get-tuple-element.336), channel_id=1, source_target_pairs={{8,0},{16,8},{24,16},{9,1},{17,9},{25,17},{10,2},{18,10},{26,18},{... | collective-permute-start | bytes 98312 | tf_op jit(solution)/shard_map/ppermute | solution.py:14
  389.8 7.0 %collective-permute-start.5 = (bf16[128,128]{1,0:T(8,128)(2,1)S(1)}, bf16[128,128]{1,0:T(8,128)(2,1)S(1)}, u32[]{:S(2)}, u32[]{:S(2)}) collective-permute-start(bf16[128,128]{1,0:T(8,128)(2,1)S(1)} %get-tuple-element.339), channel_id=1, source_target_pairs={{16,0},{24,8},{17,1},{25,9},{18,2},{26,10},{19,3},{27,11},{20,4},{... | collective-permute-start | bytes 98312 | tf_op jit(solution)/shard_map/ppermute | solution.py:14
  391.1 8.8 %collective-permute-start.6 = (bf16[128,128]{1,0:T(8,128)(2,1)S(1)}, bf16[128,128]{1,0:T(8,128)(2,1)S(1)}, u32[]{:S(2)}, u32[]{:S(2)}) collective-permute-start(bf16[128,128]{1,0:T(8,128)(2,1)S(1)} %get-tuple-element.338), channel_id=1, source_target_pairs={{24,0},{25,1},{26,2},{27,3},{28,4},{29,5},{30,6},{31,7}} | collective-permute-start | bytes 98312 | tf_op jit(solution)/shard_map/ppermute | solution.py:14
  392.4 7.5 %collective-permute-start.7 = (bf16[128,128]{1,0:T(8,128)(2,1)S(1)}, bf16[128,128]{1,0:T(8,128)(2,1)S(1)}, u32[]{:S(2)}, u32[]{:S(2)}) collective-permute-start(bf16[128,128]{1,0:T(8,128)(2,1)S(1)} %get-tuple-element.337), channel_id=1, source_target_pairs={} | collective-permute-start | bytes 98312 | tf_op jit(solution)/shard_map/ppermute | solution.py:14
Sparse Core Ops, SparseCore 0:
  78.0 69.0 all-gather.3
  149.5 56.9 all-gather.5
  269.9 57.9 reduce-scatter.1
